TPU v7x, 1024 devices: a whole 4x8x16 slice. The times are simulated.
1024 devices in a mesh: section: 64 (over y, x, core), tp: 16 (over z).
Axes of the slice: x: 4, y: 8, z: 16, core: 2. Of those that a mesh axis runs over, the one named last changes fastest.
Arguments:
- inputs: bfloat16 [64, 256, 8192], P('section', None, 'tp'), may hold values from -41 to 41, as said below
- norm_gain: bfloat16 [64, 8192], P('section', 'tp'), may hold values from 0.5 to 2
- w_value: bfloat16 [64, 8192, 512], P('section', 'tp'), may hold values from -0.0625 to 0.0625
- w_output: bfloat16 [64, 512, 8192], P('section', None, 'tp'), may hold values from -0.25 to 0.25
- moments: bfloat16 [64, 2, 8192], P('section', None, 'tp'), may hold values from 0.099609375 to 10
- capped: int32 [64], P('section'), may hold values from 0 to 1, as said below
Outputs:
- next_input: bfloat16 [64, 256, 8192], P('section', None, 'tp')
- guest_moments: bfloat16 [64, 2, 8192], P('section', None, 'tp')
Inputs may be any that keep to these rules, and one draw needn't show every extreme that they name: `capped`: each entry is 0 or 1; the last section is never capped, no two neighbouring sections are both capped, and sections 0 and 62 are always capped. `inputs`: activations of mixed row and feature scales.
All inputs are finite; a program needn't handle non-finite values.
Results may differ from a plain program's by a relative error of at most 0.0042.
Values may be sent and summed in bfloat16 or wider, within the bound.
A program may use at most 32 MiB of HBM per device.

v0:
```python
import jax
import jax.numpy as jnp
from jax import lax
from jax.sharding import PartitionSpec as P

D = 8192


eps = 1e-05


def passed_along(shard, axis, by):
    size = lax.axis_size(axis)
    pairs = [(i, i + by) for i in range(size) if 0 <= i + by < size]
    return lax.ppermute(shard, axis, pairs)


def apply_layer(stream, gain_row, w_value, w_output, active):
    widened = stream.astype(jnp.float32)
    squares = jnp.sum(widened * widened, axis=-1, keepdims=True)
    scaled = (widened * gain_row.astype(jnp.float32)).astype(jnp.bfloat16)
    projected = jnp.dot(scaled, w_value, preferred_element_type=jnp.float32)
    squares = lax.psum(squares, "tp")
    own_columns = lax.psum_scatter(projected, "tp", scatter_dimension=1, tiled=True)
    own_values = (own_columns * lax.rsqrt(squares / D + eps)).astype(jnp.bfloat16)
    values = lax.all_gather(own_values, "tp", axis=1, tiled=True)
    update = jnp.dot(values, w_output, preferred_element_type=jnp.float32)
    return (widened + active * update).astype(jnp.bfloat16)


def on_device(inputs, norm_gain, w_value, w_output, moments, capped):
    stream = inputs[0]
    own_gain = norm_gain[0]
    own_value = w_value[0]
    own_output = w_output[0]
    own_moments = moments[0]
    cap_flag = capped.astype(jnp.float32)
    received = passed_along(
        (own_value, own_output, own_gain, own_moments, capped.astype(jnp.bfloat16)), "section", 1
    )
    guest_flag = received[4].astype(jnp.float32)
    middle = apply_layer(stream, received[2], received[0], received[1], guest_flag)
    carried = received[3]
    result = apply_layer(middle, own_gain, own_value, own_output, 1.0 - cap_flag)
    next_input = passed_along(result, "section", 1)
    guest_moments = (carried.astype(jnp.float32) * guest_flag).astype(jnp.bfloat16)
    return (next_input[None], guest_moments[None])


def solution(mesh):
    return jax.shard_map(
        on_device,
        mesh=mesh,
        in_specs=(
            P("section", None, "tp"),
            P("section", "tp"),
            P("section", "tp", None),
            P("section", None, "tp"),
            P("section", None, "tp"),
            P("section"),
        ),
        out_specs=(P("section", None, "tp"), P("section", None, "tp")),
        check_vma=False,
    )
```

profile of v0, /device:TPU:33, one launch (start us, length us, event | category | flops | bytes accessed | tf_op | source)
XLA Modules:
  0.0 251.9 jit_solution(7788088624023917644)
XLA Ops:
  7.2 0.0 reduce-scatter.7.cloned.1.call-start
  7.2 3.7 %collective-permute-start.2 = (bf16[512,512]{1,0:T(8,128)(2,1)}, bf16[512,512]{1,0:T(8,128)(2,1)S(1)}, u32[]{:S(2)}, u32[]{:S(2)}) collective-permute-start(bf16[512,512]{1,0:T(8,128)(2,1)} %bitcast.42), channel_id=1, source_target_pairs={{0,16},{16,32},{32,48},{48,64},{64,80},{80,96},{96,112},{112,128},... | collective-permute-start | bytes 1572872 | tf_op jit(solution)/shard_map/ppermute | solution.py:15
  10.9 0.7 reduce
  11.6 1.9 collective-permute-start.1
  13.5 3.8 %collective-permute-done.1 = bf16[512]{0:T(512)(128)(2,1)S(1)} collective-permute-done((bf16[512]{0:T(512)(128)(2,1)S(1)}, bf16[512]{0:T(512)(128)(2,1)S(1)}, u32[]{:S(2)}, u32[]{:S(2)}) %collective-permute-start.1) | collective-permute-done | bytes 1056 | tf_op jit(solution)/shard_map/ppermute | solution.py:15
  17.3 0.0 collective-permute-done.2
  17.3 0.0 copy-start.2
  17.3 2.1 convolution_bitcast_fusion.1
  19.5 0.0 copy-start
  19.5 0.0 reduce-scatter.7.cloned.1.call-update
  19.5 0.0 reduce-scatter.9.cloned.1.call-start
  20.2 5.0 %collective-permute-start = (bf16[1]{0:T(256)(128)(2,1)}, bf16[1]{0:T(256)(128)(2,1)}, u32[]{:S(2)}, u32[]{:S(2)}) collective-permute-start(bf16[1]{0:T(256)(128)(2,1)} %convert_element_type.47), channel_id=1, source_target_pairs={{0,16},{16,32},{32,48},{48,64},{64,80},{80,96},{96,112},{112,128},... | collective-permute-start | bytes 14 | tf_op jit(solution)/shard_map/ppermute | solution.py:15
  25.3 0.0 copy-done.2
  25.3 2.0 collective-permute-start.3
  27.3 0.0 copy-done
  27.3 0.1 fusion.5
  27.4 37.6 %psum.14 = f32[256,1]{0,1:T(1,128)S(1)} all-reduce(f32[256,1]{0,1:T(1,128)S(1)} %bitcast.44), channel_id=1, replica_groups=mesh['section'=64,'tp'=16] {'tp'}, use_global_device_ids=true, to_apply=%region_2.0 | all-reduce | flops 256 | bytes 2048 | tf_op jit(solution)/shard_map/psum | solution.py:23
  65.0 0.0 collective-permute-done
  65.7 26.3 %reduce-scatter.7.cloned.1.call-done = f32[32,256]{1,0:T(8,128)} async-done(((f32[512,256]{1,0:T(8,128)}), f32[32,256]{1,0:T(8,128)}) %reduce-scatter.7.cloned.1.call-update) | async-done | bytes 32784
  92.0 0.8 fusion.13
  92.8 22.0 %all_gather.6 = bf16[256,512]{0,1:T(8,128)(2,1)S(1)} all-gather(bf16[256,32]{0,1:T(8,128)(2,1)S(1)} %fusion.13), channel_id=1, replica_groups=mesh['section'=64,'tp'=16] {'tp'}, dimensions={1}, use_global_device_ids=true | all-gather | bytes 278528 | tf_op jit(solution)/shard_map/all_gather | solution.py:26
  114.7 0.0 copy-start.1
  114.7 0.0 collective-permute-done.3
  114.7 0.4 fusion.3
  115.2 0.6 copy-done.1
  115.8 1.1 convolution_bitcast_fusion
  116.9 0.0 reduce-scatter.9.cloned.1.call-update
  116.9 21.0 %psum.15 = f32[256,1]{0,1:T(1,128)S(1)} all-reduce(f32[256,1]{0,1:T(1,128)S(1)} %bitcast.47), channel_id=1, replica_groups=mesh['section'=64,'tp'=16] {'tp'}, use_global_device_ids=true, to_apply=%region_5.0 | all-reduce | flops 256 | bytes 2048 | tf_op jit(solution)/shard_map/psum | solution.py:23
  138.0 58.0 %reduce-scatter.9.cloned.1.call-done = f32[32,256]{1,0:T(8,128)} async-done(((f32[512,256]{1,0:T(8,128)}), f32[32,256]{1,0:T(8,128)}) %reduce-scatter.9.cloned.1.call-update) | async-done | bytes 32784
  196.0 0.8 fusion.12
  196.7 21.7 %all_gather.7 = bf16[256,512]{0,1:T(8,128)(2,1)S(1)} all-gather(bf16[256,32]{0,1:T(8,128)(2,1)S(1)} %fusion.12), channel_id=1, replica_groups=mesh['section'=64,'tp'=16] {'tp'}, dimensions={1}, use_global_device_ids=true | all-gather | bytes 278528 | tf_op jit(solution)/shard_map/all_gather | solution.py:26
  218.4 0.0 copy-start.3
  218.4 0.3 fusion.1
  218.7 21.7 %collective-permute-start.4 = (bf16[256,512]{1,0:T(8,128)(2,1)S(1)}, bf16[256,512]{1,0:T(8,128)(2,1)S(1)}, u32[]{:S(2)}, u32[]{:S(2)}) collective-permute-start(bf16[256,512]{1,0:T(8,128)(2,1)S(1)} %fusion.1), channel_id=1, source_target_pairs={{0,16},{16,32},{32,48},{48,64},{64,80},{80,96},{96,112},{112,128},... | collective-permute-start | bytes 786440 | tf_op jit(solution)/shard_map/ppermute | solution.py:15
  240.5 0.0 copy-done.3
  240.5 1.9 collective-permute-start.5
  242.4 1.4 collective-permute-done.5
  243.8 0.6 fusion.14
  244.4 0.0 collective-permute-done.4
  244.4 0.7 copy.24
  (4 shorter events, 0.0 us)
Async XLA Ops:
  7.2 84.9 %reduce-scatter.7.cloned.1.call-start = ((), (), s32[]{:S(2)}) async-start(), calls=%async_computation.2 | async-start | bytes 557056
  7.2 10.1 %collective-permute-start.2 = (bf16[512,512]{1,0:T(8,128)(2,1)}, bf16[512,512]{1,0:T(8,128)(2,1)S(1)}, u32[]{:S(2)}, u32[]{:S(2)}) collective-permute-start(bf16[512,512]{1,0:T(8,128)(2,1)} %bitcast.42), channel_id=1, source_target_pairs={{0,16},{16,32},{32,48},{48,64},{64,80},{80,96},{96,112},{112,128},... | collective-permute-start | bytes 1572872 | tf_op jit(solution)/shard_map/ppermute | solution.py:15
  11.6 5.7 %collective-permute-start.1 = (bf16[512]{0:T(512)(128)(2,1)S(1)}, bf16[512]{0:T(512)(128)(2,1)S(1)}, u32[]{:S(2)}, u32[]{:S(2)}) collective-permute-start(bf16[512]{0:T(512)(128)(2,1)S(1)} %reduce), channel_id=1, source_target_pairs={{0,16},{16,32},{32,48},{48,64},{64,80},{80,96},{96,112},{112,128},... | collective-permute-start | bytes 3080 | tf_op jit(solution)/shard_map/ppermute | solution.py:15
  17.3 8.0 %copy-start.2 = (bf16[1,512,512]{2,1,0:T(8,128)(2,1)S(1)}, bf16[1,512,512]{2,1,0:T(8,128)(2,1)}, u32[]{:S(2)}) copy-start(bf16[1,512,512]{2,1,0:T(8,128)(2,1)} %param.9) | copy-start | bytes 1572868
  19.5 7.8 %copy-start = (bf16[1,256,512]{2,1,0:T(8,128)(2,1)S(1)}, bf16[1,256,512]{2,1,0:T(8,128)(2,1)}, u32[]{:S(2)}) copy-start(bf16[1,256,512]{2,1,0:T(8,128)(2,1)} %param.6) | copy-start | bytes 786436
  19.5 176.5 %reduce-scatter.9.cloned.1.call-start = ((), (), s32[]{:S(2)}) async-start(), calls=%async_computation.3 | async-start | bytes 557056
  20.2 44.8 %collective-permute-start = (bf16[1]{0:T(256)(128)(2,1)}, bf16[1]{0:T(256)(128)(2,1)}, u32[]{:S(2)}, u32[]{:S(2)}) collective-permute-start(bf16[1]{0:T(256)(128)(2,1)} %convert_element_type.47), channel_id=1, source_target_pairs={{0,16},{16,32},{32,48},{48,64},{64,80},{80,96},{96,112},{112,128},... | collective-permute-start | bytes 14 | tf_op jit(solution)/shard_map/ppermute | solution.py:15
  25.3 89.5 %collective-permute-start.3 = (bf16[512,512]{1,0:T(8,128)(2,1)S(1)}, bf16[512,512]{1,0:T(8,128)(2,1)S(1)}, u32[]{:S(2)}, u32[]{:S(2)}) collective-permute-start(bf16[512,512]{1,0:T(8,128)(2,1)S(1)} %bitcast.48), channel_id=1, source_target_pairs={{0,16},{16,32},{32,48},{48,64},{64,80},{80,96},{96,112},{112,128},... | collective-permute-start | bytes 1572872 | tf_op jit(solution)/shard_map/ppermute | solution.py:15
  114.7 1.0 copy-start.1
  218.4 22.0 %copy-start.3 = (bf16[1,2,512]{2,1,0:T(2,128)(2,1)S(1)}, bf16[1,2,512]{2,1,0:T(2,128)(2,1)}, u32[]{:S(2)}) copy-start(bf16[1,2,512]{2,1,0:T(2,128)(2,1)} %param.10) | copy-start | bytes 6148
  218.7 25.6 %collective-permute-start.4 = (bf16[256,512]{1,0:T(8,128)(2,1)S(1)}, bf16[256,512]{1,0:T(8,128)(2,1)S(1)}, u32[]{:S(2)}, u32[]{:S(2)}) collective-permute-start(bf16[256,512]{1,0:T(8,128)(2,1)S(1)} %fusion.1), channel_id=1, source_target_pairs={{0,16},{16,32},{32,48},{48,64},{64,80},{80,96},{96,112},{112,128},... | collective-permute-start | bytes 786440 | tf_op jit(solution)/shard_map/ppermute | solution.py:15
  240.5 3.3 %collective-permute-start.5 = (bf16[2,512]{1,0:T(2,128)(2,1)S(1)}, bf16[2,512]{1,0:T(2,128)(2,1)S(1)}, u32[]{:S(2)}, u32[]{:S(2)}) collective-permute-start(bf16[2,512]{1,0:T(2,128)(2,1)S(1)} %bitcast.49), channel_id=1, source_target_pairs={{0,16},{16,32},{32,48},{48,64},{64,80},{80,96},{96,112},{112,128},... | collective-permute-start | bytes 6152 | tf_op jit(solution)/shard_map/ppermute | solution.py:15
Sparse Core Ops, SparseCore 0:
  19.6 72.3 reduce-scatter.6
  117.1 78.8 reduce-scatter.8
where the time goes:
time: 256 us; the launch traced here: 252 us
  blocking collectives  102 us (40%)
  waiting for transfers between devices  89.6 us (35%)
  starting transfers between devices  36.3 us (14%)
  between operations  15.5 us (6%)
  matrix products  4.03 us (2%)
  other arithmetic  2.97 us (1%)
    unnamed x4, waiting for transfers between devices  84.4 us
    psum x2, blocking collectives, apply_layer(): squares = lax.psum(squares, 'tp')  58.6 us
    all_gather x2, blocking collectives, apply_layer(): values = lax.all_gather(own_values, 'tp', axis=1, tiled=True)  43.6 us
    ppermute x6, starting transfers between devices, passed_along(): return lax.ppermute(shard, axis, pairs)  36.3 us
    ppermute x6, waiting for transfers between devices, passed_along(): return lax.ppermute(shard, axis, pairs)  5.18 us
  transfers between devices with their start and end apart: 8, of which 4 were waited for; matrix products, arithmetic and copies ran while one was open for 1% of the time, Pallas kernels for 0%

commit v1 on v0

v1 whole, which is shorter than its diff:
```python
import functools

import jax
import jax.numpy as jnp
from jax import lax
from jax.experimental import pallas as pl
from jax.experimental.pallas import tpu as pltpu
from jax.sharding import PartitionSpec as P

MESH = pl.DeviceIdType.MESH
D = 8192
EPS = 1e-05
F32 = jnp.float32
BF16 = jnp.bfloat16

TREE = (
    (0, 6), (0, -6), (0, 3), (0, -3), (0, 1), (0, -1),
    (3, 4), (-3, -4), (3, 2), (-3, -2),
    (6, 8), (6, 7), (-6, -7), (6, 5), (-6, -5),
)
PARENT = {child: parent for parent, child in TREE}
CHILDREN = {node: [c for p, c in TREE if p == node] for node in range(-7, 9)}
RELAYS = (6, -6, 3, -3)
LEAVES = (8, 7, -7, 5, -5, 4, -4, 2, -2, 1, -1)
OFFSETS = sorted({c - p for p, c in TREE} | {p - c for p, c in TREE})


def kernel(
    tp, sections, tok, cuts,
    x_hbm, gain_ref, wv_hbm, wo_hbm, mom_ref, cap_ref,
    out_ref, gmom_ref,
    x, mid, wv, wo, wv_in, wo_in, small, small_in, scaled, values, res, *rest,
):
    chunks = len(cuts)
    channels = chunks + 1
    parts, got, relay = rest[:channels], rest[channels : 2 * channels], rest[2 * channels : 3 * channels]
    local_sem, sec_send, sec_recv, tree_send, tree_recv = rest[3 * channels :]
    me, sec = lax.axis_index("tp"), lax.axis_index("section")
    own = tok // tp
    following = lax.rem(sec + 1, sections)
    previous = lax.rem(sec + sections - 1, sections)

    def at(offset):
        return lax.rem(me + (offset + tp), tp)

    def block(offset):
        return pl.ds(pl.multiple_of(at(offset) * own, own), own)

    loads = [
        pltpu.make_async_copy(x_hbm.at[0], x, local_sem.at[0]),
        pltpu.make_async_copy(wv_hbm.at[0], wv, local_sem.at[1]),
        pltpu.make_async_copy(wo_hbm.at[0], wo, local_sem.at[2]),
    ]
    barrier = pltpu.get_barrier_semaphore()
    for offset in OFFSETS:
        pl.semaphore_signal(barrier, inc=1, device_id={"tp": at(offset)}, device_id_type=MESH)
    pl.semaphore_signal(barrier, inc=1, device_id={"section": following}, device_id_type=MESH)
    pl.semaphore_signal(barrier, inc=1, device_id={"section": previous}, device_id_type=MESH)
    for load in loads:
        load.start()
    cap = jnp.full((1, small.shape[1]), cap_ref[0].astype(F32), F32)
    small[0:1, :] = gain_ref[...].astype(F32)
    small[1:3, :] = mom_ref[0].astype(F32)
    small[3:4, :] = cap
    small[4:8, :] = jnp.zeros((4, small.shape[1]), F32)
    pl.semaphore_wait(barrier, len(OFFSETS) + 2)

    def onward(n, src, dst):
        return pltpu.make_async_remote_copy(
            src_ref=src, dst_ref=dst, send_sem=sec_send.at[n], recv_sem=sec_recv.at[n],
            device_id={"section": following}, device_id_type=MESH,
        )

    small_copy = onward(0, small, small_in)
    small_copy.start()
    wv_copies = []
    for n, (start, width) in enumerate(cuts):
        copy = onward(1 + n, wv_hbm.at[0, :, pl.ds(start, width)], wv_in.at[:, pl.ds(start, width)])
        copy.start()
        wv_copies.append(copy)
    wo_copy = onward(1 + chunks, wo_hbm.at[0], wo_in)
    wo_copy.start()

    def up(k, q, src):
        return pltpu.make_async_remote_copy(
            src_ref=src, dst_ref=got[k].at[q % tp], send_sem=tree_send.at[k, q % tp], recv_sem=tree_recv.at[k, q % tp],
            device_id={"tp": at(PARENT[q] - q)}, device_id_type=MESH,
        )

    def leaf_copy(k, q):
        return up(k, q, parts[k].at[block(-q), :])

    def leaves(k):
        for q in LEAVES:
            leaf_copy(k, q).start()

    def summed(k, p):
        total = parts[k][block(-p), :].astype(F32)
        for q in CHILDREN[p]:
            (leaf_copy(k, q) if q in LEAVES else up(k, q, relay[k].at[RELAYS.index(q)])).wait_recv()
            total = total + got[k][q % tp].astype(F32)
        return total

    def relays(k):
        for n, p in enumerate(RELAYS):
            relay[k][n] = summed(k, p).astype(BF16)
            up(k, p, relay[k].at[n]).start()

    def down(k, edge):
        p, q = edge
        rows = values.at[k - channels, block(-p), :]
        return pltpu.make_async_remote_copy(
            src_ref=rows, dst_ref=rows, send_sem=tree_send.at[k, q % tp], recv_sem=tree_recv.at[k, q % tp],
            device_id={"tp": at(q - p)}, device_id_type=MESH,
        )

    def spread(k):
        seen = {0}
        for edge in TREE:
            p = edge[0]
            if p not in seen:
                down(k, (PARENT[p], p)).wait_recv()
                seen.add(p)
            down(k, edge).start()
        for edge in TREE:
            if edge[1] not in seen:
                down(k, edge).wait_recv()

    def normalized(total, squares):
        return (total * lax.rsqrt(squares[:, 0:1] * (1.0 / D) + EPS)).astype(BF16)

    def squares_of(stream):
        return jnp.broadcast_to(jnp.sum(stream * stream, axis=-1, keepdims=True), (tok, 128))

    loads[0].wait()
    wide = x[...].astype(F32)
    first = cuts[0][1]
    parts[0][:, first:] = squares_of(wide).astype(BF16)
    small_copy.wait_recv()
    scaled[...] = (wide * small_in[0:1, :]).astype(BF16)
    guest = small_in[3:4, :] * jnp.where(sec > 0, 1.0, 0.0).astype(F32)
    gmom_ref[0] = (small_in[1:3, :] * guest).astype(BF16)
    for n, (start, width) in enumerate(cuts):
        wv_copies[n].wait_recv()
        parts[n][:, 0:width] = jnp.dot(
            scaled[...], wv_in[:, start : start + width], preferred_element_type=F32
        ).astype(BF16)
        leaves(n)
    totals = []
    for n in range(chunks):
        relays(n)
    for n in range(chunks):
        totals.append(summed(n, 0))
    squares = totals[0][:, first:]
    for n, (start, width) in enumerate(cuts):
        values[0, block(0), start : start + width] = normalized(totals[n][:, 0:width], squares)
    spread(channels)
    wo_copy.wait_recv()
    update = jnp.dot(values[0], wo_in[...], preferred_element_type=F32)
    mid[...] = (x[...].astype(F32) + guest * update).astype(BF16)

    k = chunks
    wide = mid[...].astype(F32)
    kv = wv.shape[1]
    parts[k][:, kv:] = squares_of(wide).astype(BF16)
    scaled[...] = (wide * small[0:1, :]).astype(BF16)
    loads[1].wait()
    parts[k][:, 0:kv] = jnp.dot(scaled[...], wv[...], preferred_element_type=F32).astype(BF16)
    leaves(k)
    relays(k)
    total = summed(k, 0)
    values[1, block(0), :] = normalized(total[:, 0:kv], total[:, kv:])
    spread(channels + 1)
    loads[2].wait()
    keep = sec < sections - 1
    out_copies = []
    pieces = 4
    rows = tok // pieces
    for n in range(pieces):
        span = pl.ds(n * rows, rows)
        update = jnp.dot(values[1, span, :], wo[...], preferred_element_type=F32)
        new = mid[span, :].astype(F32) + (1.0 - cap) * update
        res[span, :] = jnp.where(keep, new, 0.0).astype(BF16)
        copy = onward(2 + chunks + n, res.at[span, :], out_ref.at[0, span, :])
        copy.start()
        out_copies.append(copy)

    small_copy.wait_send()
    wo_copy.wait_send()
    for copy in wv_copies:
        copy.wait_send()
    for n in range(channels):
        for q in LEAVES:
            leaf_copy(n, q).wait_send()
        for r, p in enumerate(RELAYS):
            up(n, p, relay[n].at[r]).wait_send()
    for n in (channels, channels + 1):
        for edge in TREE:
            down(n, edge).wait_send()
    for copy in out_copies:
        copy.wait()


def on_device(tp, sections, inputs, norm_gain, w_value, w_output, moments, capped):
    tok, width = inputs.shape[1:]
    kv = w_value.shape[2]
    cuts = ((0, kv // 2), (kv // 2, kv // 2))
    widths = [w + (128 if n == 0 else 0) for n, (_, w) in enumerate(cuts)] + [kv + 128]
    channels = len(widths)
    own = tok // tp
    vmem, anywhere = pl.BlockSpec(memory_space=pltpu.VMEM), pl.BlockSpec(memory_space=pl.ANY)
    return pl.pallas_call(
        functools.partial(kernel, tp, sections, tok, cuts),
        out_shape=(
            jax.ShapeDtypeStruct(inputs.shape, BF16),
            jax.ShapeDtypeStruct(moments.shape, BF16),
        ),
        in_specs=[anywhere, vmem, anywhere, anywhere, vmem, pl.BlockSpec(memory_space=pltpu.SMEM)],
        out_specs=(anywhere, vmem),
        scratch_shapes=[
            pltpu.VMEM((tok, width), BF16),
            pltpu.VMEM((tok, width), BF16),
            pltpu.VMEM((width, kv), BF16),
            pltpu.VMEM((kv, width), BF16),
            pltpu.VMEM((width, kv), BF16),
            pltpu.VMEM((kv, width), BF16),
            pltpu.VMEM((8, width), F32),
            pltpu.VMEM((8, width), F32),
            pltpu.VMEM((tok, width), BF16),
            pltpu.VMEM((2, tok, kv), BF16),
            pltpu.VMEM((tok, width), BF16),
            *[pltpu.VMEM((tok, w), BF16) for w in widths],
            *[pltpu.VMEM((tp, own, w), BF16) for w in widths],
            *[pltpu.VMEM((len(RELAYS), own, w), BF16) for w in widths],
            pltpu.SemaphoreType.DMA((3,)),
            pltpu.SemaphoreType.DMA((channels + 5,)),
            pltpu.SemaphoreType.DMA((channels + 5,)),
            pltpu.SemaphoreType.DMA((channels + 2, tp)),
            pltpu.SemaphoreType.DMA((channels + 2, tp)),
        ],
        compiler_params=pltpu.CompilerParams(collective_id=0, has_side_effects=True),
    )(inputs, norm_gain, w_value, w_output, moments, capped)


def solution(mesh):
    return jax.shard_map(
        functools.partial(on_device, mesh.shape["tp"], mesh.shape["section"]),
        mesh=mesh,
        in_specs=(
            P("section", None, "tp"),
            P("section", "tp"),
            P("section", "tp", None),
            P("section", None, "tp"),
            P("section", None, "tp"),
            P("section"),
        ),
        out_specs=(P("section", None, "tp"), P("section", None, "tp")),
        check_vma=False,
    )
```

time: 256 us -> 83.7 us (0.33)
  the two profiles are of different devices: /device:TPU:33 before, /device:TPU:1 now
where the time goes in v1:
time: 83.7 us; the launch traced here: 83.5 us
  Pallas kernels  80 us (96%)
  local copies, waits for them, and re-layouts  2.25 us (3%)
  between operations  1.29 us (2%)
    pallas_call x1, Pallas kernels, on_device(): pl.pallas_call(functools.partial(kernel, tp, sections, tok, cuts), out_sh...  80 us
    unnamed x4, local copies, waits for them, and re-layouts  2.25 us

profile of v1, /device:TPU:1, one launch (start us, length us, event | category | flops | bytes accessed | tf_op | source)
XLA Modules:
  0.0 83.5 jit_solution(12497033446399429004)
XLA Ops:
  1.3 80.0 %shard_map.77 = (bf16[1,256,512]{2,1,0:T(8,128)(2,1)}, bf16[1,2,512]{2,1,0:T(2,128)(2,1)}) custom-call(bf16[1,256,512]{2,1,0:T(8,128)(2,1)} %x_hbm.1, bf16[1,512]{1,0:T(2,128)(2,1)} %gain_ref.1, bf16[1,512,512]{2,1,0:T(8,128)(2,1)} %wv_hbm.1, bf16[1,512,512]{2,1,0:T(8,128)(2,1)} %wo_hbm.1, bf16[1,2,512]{2,1,0:T(2,128)(2,1)} %mom_ref.1, s32[1]{0:T(128)S(6)} %copy.10.cap_ref), custom_call_target="tpu_custom_call" | custom-call | tf_op jit(solution)/shard_map/pallas_call | solution.py:212
  81.3 0.0 copy-start
  81.3 1.7 %copy.11 = bf16[1,256,512]{2,1,0:T(8,128)(2,1)} copy(bf16[1,256,512]{2,1,0:T(8,128)(2,1)} %get-tuple-element.4) | data formatting | bytes 524288
  83.0 0.0 copy-done
  83.0 0.6 copy.12
Async XLA Ops:
  81.3 1.7 %copy-start = (bf16[1,2,512]{2,1,0:T(2,128)(2,1)S(1)}, bf16[1,2,512]{2,1,0:T(2,128)(2,1)}, u32[]{:S(2)}) copy-start(bf16[1,2,512]{2,1,0:T(2,128)(2,1)} %get-tuple-element.5) | copy-start | bytes 6148

commit v2 on v0

v2 whole, which is shorter than its diff:
```python
import functools

import jax
import jax.numpy as jnp
from jax import lax
from jax.experimental import pallas as pl
from jax.experimental.pallas import tpu as pltpu
from jax.sharding import PartitionSpec as P

MESH = pl.DeviceIdType.MESH
D = 8192
EPS = 1e-05
F32 = jnp.float32
BF16 = jnp.bfloat16

TREE = (
    (0, 6), (0, -6), (0, 3), (0, -3), (0, 1), (0, -1),
    (3, 4), (-3, -4), (3, 2), (-3, -2),
    (6, 8), (6, 7), (-6, -7), (6, 5), (-6, -5),
)
PARENT = {child: parent for parent, child in TREE}
CHILDREN = {node: [c for p, c in TREE if p == node] for node in range(-7, 9)}
RELAYS = (6, -6, 3, -3)
LEAVES = (8, 7, -7, 5, -5, 4, -4, 2, -2, 1, -1)
NEAR, FAR = (-3, -2, -1, 0, 1, 2, 3, 4), (5, 6, 7, 8, -7, -6, -5, -4)
ORDER = NEAR + FAR
OFFSETS = sorted({c - p for p, c in TREE} | {p - c for p, c in TREE})


def kernel(
    tp, sections, tok,
    x_hbm, gain_hbm, wv_hbm, wo_hbm, mom_hbm, cap_hbm,
    out_ref, gmom_ref,
    x, guest, mid, wv, wo, values, res, gain_ref, mom_ref, cap_ref, gmom, *rest,
):
    parts, got, relay = rest[0:2], rest[2:4], rest[4:6]
    local_sem, send_sem, recv_sem, mid_send, mid_recv, out_send, out_recv, tree_send, tree_recv = rest[6:]
    me, sec = lax.axis_index("tp"), lax.axis_index("section")
    own = tok // tp
    kv = wv.shape[1]
    following = lax.rem(sec + 1, sections)
    previous = lax.rem(sec + sections - 1, sections)

    def at(offset):
        return lax.rem(me + (offset + tp), tp)

    def block(q):
        return pl.ds(pl.multiple_of(at(-q) * own, own), own)

    def slot(q):
        return pl.ds(ORDER.index(q) * own, own)

    def span(group):
        return pl.ds(ORDER.index(group[0]) * own, len(group) * own)

    def onward(src, dst, send, recv):
        return pltpu.make_async_remote_copy(
            src_ref=src, dst_ref=dst, send_sem=send, recv_sem=recv,
            device_id={"section": following}, device_id_type=MESH,
        )

    x_loads = [pltpu.make_async_copy(x_hbm.at[0, block(q), :], x.at[slot(q), :], local_sem.at[n]) for n, q in enumerate(ORDER)]
    loads = [
        pltpu.make_async_copy(wv_hbm.at[0], wv, local_sem.at[tp]),
        pltpu.make_async_copy(wo_hbm.at[0], wo, local_sem.at[tp + 1]),
    ]
    smalls = [
        pltpu.make_async_copy(gain_hbm, gain_ref, local_sem.at[tp + 2]),
        pltpu.make_async_copy(mom_hbm, mom_ref, local_sem.at[tp + 3]),
        pltpu.make_async_copy(cap_hbm, cap_ref, local_sem.at[tp + 4]),
    ]
    first, last = sec == 0, sec == sections - 1
    inner, outer = jnp.logical_not(first), jnp.logical_not(last)
    barrier = pltpu.get_barrier_semaphore()

    @pl.when(outer)
    def _():
        pl.semaphore_signal(barrier, inc=1, device_id={"section": following}, device_id_type=MESH)

    @pl.when(inner)
    def _():
        pl.semaphore_signal(barrier, inc=1, device_id={"section": previous}, device_id_type=MESH)

    for offset in OFFSETS:
        pl.semaphore_signal(barrier, inc=1, device_id={"tp": at(offset)}, device_id_type=MESH)
    for load in x_loads + smalls + loads:
        load.start()
    for load in x_loads:
        load.wait()

    @pl.when(jnp.logical_or(first, last))
    def _():
        pl.semaphore_wait(barrier, len(OFFSETS) + 1)

    @pl.when(jnp.logical_and(inner, outer))
    def _():
        pl.semaphore_wait(barrier, len(OFFSETS) + 2)

    def guest_copy(n, group):
        return pltpu.make_async_remote_copy(
            src_ref=x.at[span(group), :], dst_ref=guest.at[span(group), :], send_sem=send_sem.at[n], recv_sem=recv_sem.at[n],
            device_id={"section": previous}, device_id_type=MESH,
        )

    guest_copies = [guest_copy(n, group) for n, group in enumerate((FAR, NEAR))]

    @pl.when(inner)
    def _():
        for copy in guest_copies:
            copy.start()

    for load in smalls:
        load.wait()
    cap = jnp.full((1, x.shape[1]), cap_ref[0].astype(F32), F32)
    gain = gain_ref[...].astype(F32)
    gmom[...] = (mom_ref[0].astype(F32) * cap).astype(BF16)
    gmom_copy = onward(gmom, gmom_ref.at[0], send_sem.at[2], recv_sem.at[2])

    @pl.when(outer)
    def _():
        gmom_copy.start()

    @pl.when(first)
    def _():
        mid[...] = x[...]
        out_ref[...] = jnp.zeros_like(out_ref)
        gmom_ref[...] = jnp.zeros_like(gmom_ref)

    @pl.when(last)
    def _():
        guest[...] = x[...]

    def up(k, q, src):
        return pltpu.make_async_remote_copy(
            src_ref=src, dst_ref=got[k].at[q % tp], send_sem=tree_send.at[k, q % tp], recv_sem=tree_recv.at[k, q % tp],
            device_id={"tp": at(PARENT[q] - q)}, device_id_type=MESH,
        )

    def leaf_copy(k, q):
        return up(k, q, parts[k].at[slot(q), :])

    def down(k, edge):
        p, q = edge
        return pltpu.make_async_remote_copy(
            src_ref=values.at[k, slot(p), :], dst_ref=values.at[k, slot(q), :],
            send_sem=tree_send.at[2 + k, q % tp], recv_sem=tree_recv.at[2 + k, q % tp],
            device_id={"tp": at(q - p)}, device_id_type=MESH,
        )

    def project(k, group, stream):
        rows = span(group)
        total = jnp.sum(stream * stream, axis=-1, keepdims=True)
        parts[k][rows, kv:] = jnp.broadcast_to(total, (stream.shape[0], 128)).astype(BF16)
        parts[k][rows, 0:kv] = jnp.dot(
            (stream * gain).astype(BF16), wv[...], preferred_element_type=F32
        ).astype(BF16)
        for q in group:
            if q in LEAVES:
                leaf_copy(k, q).start()

    def summed(k, p):
        total = parts[k][slot(p), :].astype(F32)
        for q in CHILDREN[p]:
            (leaf_copy(k, q) if q in LEAVES else up(k, q, relay[k].at[RELAYS.index(q)])).wait_recv()
            total = total + got[k][q % tp].astype(F32)
        return total

    def gather(k, order):
        for p in order:
            n = RELAYS.index(p)
            relay[k][n] = summed(k, p).astype(BF16)
            up(k, p, relay[k].at[n]).start()
        total = summed(k, 0)
        squares = total[:, kv : kv + 1]
        values[k, slot(0), :] = (total[:, 0:kv] * lax.rsqrt(squares * (1.0 / D) + EPS)).astype(BF16)

    def spread(k):
        seen = {0}
        for edge in TREE:
            p = edge[0]
            if p not in seen:
                down(k, (PARENT[p], p)).wait_recv()
                seen.add(p)
            down(k, edge).start()
        return seen

    def updated(k, group, seen):
        for q in group:
            if q not in seen:
                down(k, (PARENT[q], q)).wait_recv()
        return jnp.dot(values[k, span(group), :], wo[...], preferred_element_type=F32)

    loads[0].wait()
    for copy, group in zip(guest_copies, (FAR, NEAR)):

        @pl.when(outer)
        def _():
            copy.wait_recv()

        project(0, group, guest[span(group), :].astype(F32))
    gather(0, RELAYS)
    seen = spread(0)
    loads[1].wait()
    mid_copies = []
    for n, group in enumerate((NEAR, FAR)):
        rows = span(group)
        update = updated(0, group, seen)
        res[0, rows, :] = (guest[rows, :].astype(F32) + cap * update).astype(BF16)
        copy = onward(res.at[0, rows, :], mid.at[rows, :], mid_send.at[n], mid_recv.at[n])
        mid_copies.append(copy)

        @pl.when(outer)
        def _():
            copy.start()

    for copy, group in zip(mid_copies, (NEAR, FAR)):

        @pl.when(inner)
        def _():
            copy.wait_recv()

        project(1, group, mid[span(group), :].astype(F32))
    gather(1, RELAYS[2:] + RELAYS[:2])
    seen = spread(1)
    out_copies = []
    for group in (NEAR, FAR):
        rows = span(group)
        update = updated(1, group, seen)
        res[1, rows, :] = (mid[rows, :].astype(F32) + (1.0 - cap) * update).astype(BF16)
        copies = [
            onward(res.at[1, slot(q), :], out_ref.at[0, block(q), :], out_send.at[ORDER.index(q)], out_recv.at[ORDER.index(q)])
            for q in group
        ]
        out_copies += copies

        @pl.when(outer)
        def _():
            for copy in copies:
                copy.start()

    @pl.when(outer)
    def _():
        for copy in [gmom_copy, *mid_copies, *out_copies]:
            copy.wait_send()

    @pl.when(inner)
    def _():
        for copy in guest_copies:
            copy.wait_send()

    for k in (0, 1):
        for q in LEAVES:
            leaf_copy(k, q).wait_send()
        for n, p in enumerate(RELAYS):
            up(k, p, relay[k].at[n]).wait_send()
        for edge in TREE:
            down(k, edge).wait_send()

    @pl.when(inner)
    def _():
        for copy in [gmom_copy, *out_copies]:
            copy.wait_recv()


def on_device(tp, sections, inputs, norm_gain, w_value, w_output, moments, capped):
    tok, width = inputs.shape[1:]
    kv = w_value.shape[2]
    own = tok // tp
    vmem, anywhere = pl.BlockSpec(memory_space=pltpu.VMEM), pl.BlockSpec(memory_space=pl.ANY)
    stream = pltpu.VMEM((tok, width), BF16)
    copies = pltpu.SemaphoreType.DMA
    return pl.pallas_call(
        functools.partial(kernel, tp, sections, tok),
        out_shape=(pltpu.VMEM(inputs.shape, BF16), pltpu.VMEM(moments.shape, BF16)),
        in_specs=[anywhere] * 6,
        out_specs=(vmem, vmem),
        scratch_shapes=[
            stream,
            stream,
            stream,
            pltpu.VMEM((width, kv), BF16),
            pltpu.VMEM((kv, width), BF16),
            pltpu.VMEM((2, tok, kv), BF16),
            pltpu.VMEM((2, tok, width), BF16),
            pltpu.VMEM(norm_gain.shape, BF16),
            pltpu.VMEM(moments.shape, BF16),
            pltpu.SMEM(capped.shape, jnp.int32),
            pltpu.VMEM(moments.shape[1:], BF16),
            *[pltpu.VMEM((tok, kv + 128), BF16)] * 2,
            *[pltpu.VMEM((tp, own, kv + 128), BF16)] * 2,
            *[pltpu.VMEM((len(RELAYS), own, kv + 128), BF16)] * 2,
            copies((tp + 5,)),
            copies((3,)),
            copies((3,)),
            copies((2,)),
            copies((2,)),
            copies((tp,)),
            copies((tp,)),
            copies((4, tp)),
            copies((4, tp)),
        ],
        compiler_params=pltpu.CompilerParams(collective_id=0, has_side_effects=True),
    )(inputs, norm_gain, w_value, w_output, moments, capped)


def solution(mesh):
    return jax.shard_map(
        functools.partial(on_device, mesh.shape["tp"], mesh.shape["section"]),
        mesh=mesh,
        in_specs=(
            P("section", None, "tp"),
            P("section", "tp"),
            P("section", "tp", None),
            P("section", None, "tp"),
            P("section", None, "tp"),
            P("section"),
        ),
        out_specs=(P("section", None, "tp"), P("section", None, "tp")),
        check_vma=False,
    )
```

time: 256 us -> 76.6 us (0.30); the launches traced: 252 us -> 76.1 us
  blocking collectives: 102 us -> 0 us
  waiting for transfers between devices: 89.6 us -> 0 us
  Pallas kernels: 0 us -> 73.5 us
  starting transfers between devices: 36.3 us -> 0 us
  between operations: 15.5 us -> 1.29 us
  matrix products: 4.03 us -> 0 us
  other arithmetic: 2.97 us -> 0 us
    unnamed x4 -> x0, waiting for transfers between devices: 84.4 us -> none
    pallas_call x0 -> x1, Pallas kernels: none -> 73.5 us  [on_device(): pl.pallas_call(functools.partial(kernel, tp, sections, tok), out_shape=(p...]
    psum x2 -> x0, blocking collectives: 58.6 us -> none  [apply_layer(): squares = lax.psum(squares, 'tp')]
    all_gather x2 -> x0, blocking collectives: 43.6 us -> none  [apply_layer(): values = lax.all_gather(own_values, 'tp', axis=1, tiled=True)]
    ppermute x6 -> x0, starting transfers between devices: 36.3 us -> none  [passed_along(): return lax.ppermute(shard, axis, pairs)]
    ppermute x6 -> x0, waiting for transfers between devices: 5.18 us -> none  [passed_along(): return lax.ppermute(shard, axis, pairs)]
    unnamed x2 -> x0, matrix products: 3.28 us -> none
  transfers between devices with their start and end apart: 8 -> 0, of which waited for: 4 -> 0; matrix products, arithmetic and copies ran while one was open for 1% -> 0% of each run, Pallas kernels for 0% -> 0%
where the time goes in v2:
time: 76.6 us; the launch traced here: 76.1 us
  Pallas kernels  73.5 us (96%)
  between operations  1.29 us (2%)
  local copies, waits for them, and re-layouts  1.28 us (2%)
    pallas_call x1, Pallas kernels, on_device(): pl.pallas_call(functools.partial(kernel, tp, sections, tok), out_shape=(p...  73.5 us

profile of v2, /device:TPU:33, one launch (start us, length us, event | category | flops | bytes accessed | tf_op | source)
XLA Modules:
  0.0 76.1 jit_solution(7705995465663910018)
XLA Ops:
  1.3 73.5 %shard_map.77 = (bf16[1,256,512]{2,1,0:T(8,128)(2,1)S(1)}, bf16[1,2,512]{2,1,0:T(2,128)(2,1)S(1)}) custom-call(bf16[1,256,512]{2,1,0:T(8,128)(2,1)} %x_hbm.1, bf16[1,512]{1,0:T(2,128)(2,1)} %gain_hbm.1, bf16[1,512,512]{2,1,0:T(8,128)(2,1)} %wv_hbm.1, bf16[1,512,512]{2,1,0:T(8,128)(2,1)} %wo_hbm.1, bf16[1,2,512]{2,1,0:T(2,128)(2,1)} %mom_hbm.1, ...), custom_call_target="tpu_custom_call" | custom-call | tf_op jit(solution)/shard_map/pallas_call | solution.py:272
  74.8 0.7 copy.10
  75.5 0.6 copy.11

commit v3 on v2

v3 whole, which is shorter than its diff:
```python
import functools

import jax
import jax.numpy as jnp
from jax import lax
from jax.experimental import pallas as pl
from jax.experimental.pallas import tpu as pltpu
from jax.sharding import PartitionSpec as P

MESH = pl.DeviceIdType.MESH
D = 8192
EPS = 1e-05
F32 = jnp.float32
BF16 = jnp.bfloat16

TREE = (
    (0, 6), (0, -6), (0, 3), (0, -3), (0, 1), (0, -1),
    (3, 4), (-3, -4), (3, 2), (-3, -2),
    (6, 8), (6, 7), (-6, -7), (6, 5), (-6, -5),
)
PARENT = {child: parent for parent, child in TREE}
CHILDREN = {node: [c for p, c in TREE if p == node] for node in range(-7, 9)}
RELAYS = (6, -6, 3, -3)
LEAVES = (8, 7, -7, 5, -5, 4, -4, 2, -2, 1, -1)
NEAR, FAR = (-3, -2, -1, 0, 1, 2, 3, 4), (5, 6, 7, 8, -7, -6, -5, -4)
ORDER = NEAR + FAR
HEADS = (6, -6, 3, -3, 1, -1, 0)
OFFSETS = sorted({c - p for p, c in TREE} | {p - c for p, c in TREE})


def kernel(
    tp, sections, tok,
    x_hbm, gain_hbm, wv_hbm, wo_hbm, mom_hbm, cap_hbm,
    out_ref, gmom_ref,
    x, guest, mid, mid_in, wv, wo_in, owned, values, gain_ref, mom_ref, cap_ref, gmom, flag, flag_in, *rest,
):
    parts, got, relay = rest[0:2], rest[2:4], rest[4:6]
    local_sem, send_sem, recv_sem, tree_send, tree_recv = rest[6:]
    me, sec = lax.axis_index("tp"), lax.axis_index("section")
    own = tok // tp
    kv = wv.shape[1]
    following = lax.rem(sec + 1, sections)
    previous = lax.rem(sec + sections - 1, sections)
    first, last = sec == 0, sec == sections - 1
    inner, outer = jnp.logical_not(first), jnp.logical_not(last)

    def at(offset):
        return lax.rem(me + (offset + tp), tp)

    def block(q):
        return pl.ds(pl.multiple_of(at(-q) * own, own), own)

    def slot(q):
        return pl.ds(ORDER.index(q) * own, own)

    def span(group):
        return pl.ds(ORDER.index(group[0]) * own, len(group) * own)

    def beside(n, src, dst, section):
        return pltpu.make_async_remote_copy(
            src_ref=src, dst_ref=dst, send_sem=send_sem.at[n], recv_sem=recv_sem.at[n],
            device_id={"section": section}, device_id_type=MESH,
        )

    x_loads = [pltpu.make_async_copy(x_hbm.at[0, block(q), :], x.at[slot(q), :], local_sem.at[n]) for n, q in enumerate(ORDER)]
    wv_load = pltpu.make_async_copy(wv_hbm.at[0], wv, local_sem.at[tp])
    smalls = [
        pltpu.make_async_copy(gain_hbm, gain_ref, local_sem.at[tp + 1]),
        pltpu.make_async_copy(mom_hbm, mom_ref, local_sem.at[tp + 2]),
        pltpu.make_async_copy(cap_hbm, cap_ref, local_sem.at[tp + 3]),
    ]
    barrier = pltpu.get_barrier_semaphore()

    @pl.when(inner)
    def _():
        for p in HEADS[::-1]:
            pl.semaphore_signal(barrier, inc=1, device_id={"section": previous, "tp": at(-p)}, device_id_type=MESH)

    @pl.when(outer)
    def _():
        for p in HEADS[::-1]:
            pl.semaphore_signal(barrier, inc=1, device_id={"section": following, "tp": at(p)}, device_id_type=MESH)

    for offset in OFFSETS:
        pl.semaphore_signal(barrier, inc=1, device_id={"tp": at(offset)}, device_id_type=MESH)
    for load in [*x_loads, wv_load, *smalls]:
        load.start()
    for load in x_loads:
        load.wait()

    @pl.when(jnp.logical_or(first, last))
    def _():
        pl.semaphore_wait(barrier, len(OFFSETS) + len(HEADS))

    @pl.when(jnp.logical_and(inner, outer))
    def _():
        pl.semaphore_wait(barrier, len(OFFSETS) + 2 * len(HEADS))

    guest_copies = [beside(n, x.at[span(g), :], guest.at[span(g), :], previous) for n, g in enumerate((FAR, NEAR))]

    @pl.when(inner)
    def _():
        for copy in guest_copies:
            copy.start()

    wo_copy = beside(2, wo_hbm.at[0], wo_in, following)

    @pl.when(outer)
    def _():
        wo_copy.start()

    for load in smalls:
        load.wait()
    cap = jnp.full(flag.shape, cap_ref[0].astype(F32), F32)
    flag[...] = cap
    gain = gain_ref[...].astype(F32)
    gmom[...] = (mom_ref[0].astype(F32) * cap[0:1, :]).astype(BF16)
    small_copies = [beside(3, flag, flag_in, following), beside(4, gmom, gmom_ref.at[0], following)]

    @pl.when(outer)
    def _():
        for copy in small_copies:
            copy.start()

    @pl.when(first)
    def _():
        mid[...] = x[...]
        out_ref[...] = jnp.zeros_like(out_ref)
        gmom_ref[...] = jnp.zeros_like(gmom_ref)

    @pl.when(last)
    def _():
        guest[...] = x[...]

    def up(k, q, src):
        return pltpu.make_async_remote_copy(
            src_ref=src, dst_ref=got[k].at[q % tp], send_sem=tree_send.at[k, q % tp], recv_sem=tree_recv.at[k, q % tp],
            device_id={"tp": at(PARENT[q] - q)}, device_id_type=MESH,
        )

    def leaf_copy(k, q):
        return up(k, q, parts[k].at[slot(q), :])

    def lead(k, q):
        return pltpu.make_async_remote_copy(
            src_ref=owned.at[k], dst_ref=values.at[k, slot(q), :],
            send_sem=tree_send.at[2 + k, q % tp], recv_sem=tree_recv.at[2 + k, q % tp],
            device_id={"section": following, "tp": at(q)}, device_id_type=MESH,
        )

    def down(k, edge):
        p, q = edge
        return pltpu.make_async_remote_copy(
            src_ref=values.at[k, slot(p), :], dst_ref=values.at[k, slot(q), :],
            send_sem=tree_send.at[2 + k, q % tp], recv_sem=tree_recv.at[2 + k, q % tp],
            device_id={"tp": at(q - p)}, device_id_type=MESH,
        )

    def project(k, group, stream):
        rows = span(group)
        total = jnp.sum(stream * stream, axis=-1, keepdims=True)
        parts[k][rows, kv:] = jnp.broadcast_to(total, (stream.shape[0], 128)).astype(BF16)
        parts[k][rows, 0:kv] = jnp.dot(
            (stream * gain).astype(BF16), wv[...], preferred_element_type=F32
        ).astype(BF16)
        for q in group:
            if q in LEAVES:
                leaf_copy(k, q).start()

    def summed(k, p):
        total = parts[k][slot(p), :].astype(F32)
        for q in CHILDREN[p]:
            (leaf_copy(k, q) if q in LEAVES else up(k, q, relay[k].at[RELAYS.index(q)])).wait_recv()
            total = total + got[k][q % tp].astype(F32)
        return total

    def pass_on(k, order):
        for p in order:
            n = RELAYS.index(p)
            relay[k][n] = summed(k, p).astype(BF16)
            up(k, p, relay[k].at[n]).start()

    def own_values(k):
        total = summed(k, 0)
        squares = total[:, kv : kv + 1]
        owned[k] = (total[:, 0:kv] * lax.rsqrt(squares * (1.0 / D) + EPS)).astype(BF16)

        @pl.when(outer)
        def _():
            for q in HEADS:
                lead(k, q).start()

    def forward(k):
        for p in RELAYS[2:] + RELAYS[:2]:
            lead(k, p).wait_recv()
            for q in CHILDREN[p]:
                down(k, (p, q)).start()

    def updated(k, group):
        for q in group:
            if q in HEADS:
                if q not in RELAYS:
                    lead(k, q).wait_recv()
            else:
                down(k, (PARENT[q], q)).wait_recv()
        return jnp.dot(values[k, span(group), :], wo_in[...], preferred_element_type=F32)

    wv_load.wait()
    for copy, group in zip(guest_copies, (FAR, NEAR)):

        @pl.when(outer)
        def _():
            copy.wait_recv()

        project(0, group, guest[span(group), :].astype(F32))
    pass_on(0, RELAYS)
    own_values(0)

    mid_copies = [beside(5 + n, mid.at[span(g), :], mid_in.at[span(g), :], following) for n, g in enumerate((NEAR, FAR))]

    @pl.when(inner)
    def _():
        forward(0)
        wo_copy.wait_recv()
        small_copies[0].wait_recv()

    for group in (NEAR, FAR):
        rows = span(group)

        @pl.when(inner)
        def _():
            mid[rows, :] = (x[rows, :].astype(F32) + flag_in[0:1, :] * updated(0, group)).astype(BF16)

        project(1, group, mid[rows, :].astype(F32))
        if group == NEAR:

            @pl.when(outer)
            def _():
                mid_copies[0].start()

    pass_on(1, RELAYS[2:] + RELAYS[:2])

    @pl.when(outer)
    def _():
        mid_copies[1].start()

    own_values(1)

    @pl.when(inner)
    def _():
        forward(1)
        for copy, group in zip(mid_copies, (NEAR, FAR)):
            copy.wait_recv()
            rows = span(group)
            new = mid_in[rows, :].astype(F32) + (1.0 - flag_in[0:1, :]) * updated(1, group)
            new = new.astype(BF16)
            for n, q in enumerate(group):
                out_ref[0, block(q), :] = new[n * own : (n + 1) * own, :]
        small_copies[1].wait_recv()
        for copy in guest_copies:
            copy.wait_send()
        for k in (0, 1):
            for p, q in TREE:
                if p != 0:
                    down(k, (p, q)).wait_send()

    @pl.when(outer)
    def _():
        for copy in [wo_copy, *small_copies, *mid_copies]:
            copy.wait_send()
        for k in (0, 1):
            for q in HEADS:
                lead(k, q).wait_send()

    for k in (0, 1):
        for q in LEAVES:
            leaf_copy(k, q).wait_send()
        for n, p in enumerate(RELAYS):
            up(k, p, relay[k].at[n]).wait_send()


def on_device(tp, sections, inputs, norm_gain, w_value, w_output, moments, capped):
    tok, width = inputs.shape[1:]
    kv = w_value.shape[2]
    own = tok // tp
    vmem, anywhere = pl.BlockSpec(memory_space=pltpu.VMEM), pl.BlockSpec(memory_space=pl.ANY)
    stream = pltpu.VMEM((tok, width), BF16)
    copies = pltpu.SemaphoreType.DMA
    return pl.pallas_call(
        functools.partial(kernel, tp, sections, tok),
        out_shape=(pltpu.VMEM(inputs.shape, BF16), pltpu.VMEM(moments.shape, BF16)),
        in_specs=[anywhere] * 6,
        out_specs=(vmem, vmem),
        scratch_shapes=[
            *[stream] * 4,
            pltpu.VMEM((width, kv), BF16),
            pltpu.VMEM((kv, width), BF16),
            pltpu.VMEM((2, own, kv), BF16),
            pltpu.VMEM((2, tok, kv), BF16),
            pltpu.VMEM(norm_gain.shape, BF16),
            pltpu.VMEM(moments.shape, BF16),
            pltpu.SMEM(capped.shape, jnp.int32),
            pltpu.VMEM(moments.shape[1:], BF16),
            *[pltpu.VMEM((8, width), F32)] * 2,
            *[pltpu.VMEM((tok, kv + 128), BF16)] * 2,
            *[pltpu.VMEM((tp, own, kv + 128), BF16)] * 2,
            *[pltpu.VMEM((len(RELAYS), own, kv + 128), BF16)] * 2,
            copies((tp + 4,)),
            copies((7,)),
            copies((7,)),
            copies((4, tp)),
            copies((4, tp)),
        ],
        compiler_params=pltpu.CompilerParams(collective_id=0, has_side_effects=True),
    )(inputs, norm_gain, w_value, w_output, moments, capped)


def solution(mesh):
    return jax.shard_map(
        functools.partial(on_device, mesh.shape["tp"], mesh.shape["section"]),
        mesh=mesh,
        in_specs=(
            P("section", None, "tp"),
            P("section", "tp"),
            P("section", "tp", None),
            P("section", None, "tp"),
            P("section", None, "tp"),
            P("section"),
        ),
        out_specs=(P("section", None, "tp"), P("section", None, "tp")),
        check_vma=False,
    )
```

time: 76.6 us -> 75.1 us (0.980)
  the two profiles are of different devices: /device:TPU:33 before, /device:TPU:49 now
where the time goes in v3:
time: 75.1 us; the launch traced here: 74.9 us
  Pallas kernels  72.3 us (96%)
  between operations  1.29 us (2%)
  local copies, waits for them, and re-layouts  1.28 us (2%)
    pallas_call x1, Pallas kernels, on_device(): pl.pallas_call(functools.partial(kernel, tp, sections, tok), out_shape=(p...  72.3 us

profile of v3, /device:TPU:49, one launch (start us, length us, event | category | flops | bytes accessed | tf_op | source)
XLA Modules:
  0.0 74.9 jit_solution(7621310379434850685)
XLA Ops:
  1.3 72.3 %shard_map.77 = (bf16[1,256,512]{2,1,0:T(8,128)(2,1)S(1)}, bf16[1,2,512]{2,1,0:T(2,128)(2,1)S(1)}) custom-call(bf16[1,256,512]{2,1,0:T(8,128)(2,1)} %x_hbm.1, bf16[1,512]{1,0:T(2,128)(2,1)} %gain_hbm.1, bf16[1,512,512]{2,1,0:T(8,128)(2,1)} %wv_hbm.1, bf16[1,512,512]{2,1,0:T(8,128)(2,1)} %wo_hbm.1, bf16[1,2,512]{2,1,0:T(2,128)(2,1)} %mom_hbm.1, ...), custom_call_target="tpu_custom_call" | custom-call | tf_op jit(solution)/shard_map/pallas_call | solution.py:289
  73.6 0.7 copy.10
  74.3 0.6 copy.11

commit v4 on v3

--- a/solution.py
+++ b/solution.py
@@ -14,17 +14,17 @@
 BF16 = jnp.bfloat16
 
 TREE = (
-    (0, 6), (0, -6), (0, 3), (0, -3), (0, 1), (0, -1),
-    (3, 4), (-3, -4), (3, 2), (-3, -2),
-    (6, 8), (6, 7), (-6, -7), (6, 5), (-6, -5),
+    (0, 5), (0, -5), (0, 2), (0, -2), (0, 1), (0, -1),
+    (2, 3), (-2, -3),
+    (5, 8), (5, 7), (-5, -7), (5, 6), (-5, -6), (5, 4), (-5, -4),
 )
 PARENT = {child: parent for parent, child in TREE}
 CHILDREN = {node: [c for p, c in TREE if p == node] for node in range(-7, 9)}
-RELAYS = (6, -6, 3, -3)
-LEAVES = (8, 7, -7, 5, -5, 4, -4, 2, -2, 1, -1)
+RELAYS = (5, -5, 2, -2)
+LEAVES = (8, 7, -7, 6, -6, 4, -4, 3, -3, 1, -1)
 NEAR, FAR = (-3, -2, -1, 0, 1, 2, 3, 4), (5, 6, 7, 8, -7, -6, -5, -4)
 ORDER = NEAR + FAR
-HEADS = (6, -6, 3, -3, 1, -1, 0)
+HEADS = (5, -5, 2, -2, 1, -1, 0)
 OFFSETS = sorted({c - p for p, c in TREE} | {p - c for p, c in TREE})
 
 
@@ -224,7 +224,7 @@
         wo_copy.wait_recv()
         small_copies[0].wait_recv()
 
-    for group in (NEAR, FAR):
+    for group in (NEAR, FAR[:4], FAR[4:]):
         rows = span(group)
 
         @pl.when(inner)

time: 75.1 us -> 72.9 us (0.971)
  the two profiles are of different devices: /device:TPU:49 before, /device:TPU:41 now
where the time goes in v4:
time: 72.9 us; the launch traced here: 72.7 us
  Pallas kernels  70.1 us (96%)
  between operations  1.29 us (2%)
  local copies, waits for them, and re-layouts  1.28 us (2%)
    pallas_call x1, Pallas kernels, on_device(): pl.pallas_call(functools.partial(kernel, tp, sections, tok), out_shape=(p...  70.1 us

profile of v4, /device:TPU:41, one launch (start us, length us, event | category | flops | bytes accessed | tf_op | source)
XLA Modules:
  0.0 72.7 jit_solution(2214441199746184831)
XLA Ops:
  1.3 70.1 %shard_map.77 = (bf16[1,256,512]{2,1,0:T(8,128)(2,1)S(1)}, bf16[1,2,512]{2,1,0:T(2,128)(2,1)S(1)}) custom-call(bf16[1,256,512]{2,1,0:T(8,128)(2,1)} %x_hbm.1, bf16[1,512]{1,0:T(2,128)(2,1)} %gain_hbm.1, bf16[1,512,512]{2,1,0:T(8,128)(2,1)} %wv_hbm.1, bf16[1,512,512]{2,1,0:T(8,128)(2,1)} %wo_hbm.1, bf16[1,2,512]{2,1,0:T(2,128)(2,1)} %mom_hbm.1, ...), custom_call_target="tpu_custom_call" | custom-call | tf_op jit(solution)/shard_map/pallas_call | solution.py:289
  71.4 0.7 copy.10
  72.1 0.6 copy.11

commit v5 on v4

--- a/solution.py
+++ b/solution.py
@@ -15,8 +15,8 @@
 
 TREE = (
     (0, 5), (0, -5), (0, 2), (0, -2), (0, 1), (0, -1),
-    (2, 3), (-2, -3),
-    (5, 8), (5, 7), (-5, -7), (5, 6), (-5, -6), (5, 4), (-5, -4),
+    (2, 4), (-2, -4), (2, 3), (-2, -3),
+    (5, 8), (5, 7), (-5, -7), (5, 6), (-5, -6),
 )
 PARENT = {child: parent for parent, child in TREE}
 CHILDREN = {node: [c for p, c in TREE if p == node] for node in range(-7, 9)}
@@ -96,7 +96,7 @@
     def _():
         pl.semaphore_wait(barrier, len(OFFSETS) + 2 * len(HEADS))
 
-    guest_copies = [beside(n, x.at[span(g), :], guest.at[span(g), :], previous) for n, g in enumerate((FAR, NEAR))]
+    guest_copies = [beside(n, x.at[span(g), :], guest.at[span(g), :], previous) for n, g in ((0, FAR[:4]), (1, FAR[4:]), (7, NEAR))]
 
     @pl.when(inner)
     def _():
@@ -206,7 +206,7 @@
         return jnp.dot(values[k, span(group), :], wo_in[...], preferred_element_type=F32)
 
     wv_load.wait()
-    for copy, group in zip(guest_copies, (FAR, NEAR)):
+    for copy, group in zip(guest_copies, (FAR[:4], FAR[4:], NEAR)):
 
         @pl.when(outer)
         def _():
@@ -306,8 +306,8 @@
             *[pltpu.VMEM((tp, own, kv + 128), BF16)] * 2,
             *[pltpu.VMEM((len(RELAYS), own, kv + 128), BF16)] * 2,
             copies((tp + 4,)),
-            copies((7,)),
-            copies((7,)),
+            copies((8,)),
+            copies((8,)),
             copies((4, tp)),
             copies((4, tp)),
         ],

time: 72.9 us -> 72.6 us (level)
  the two profiles are of different devices: /device:TPU:41 before, /device:TPU:33 now
where the time goes in v5:
time: 72.6 us; the launch traced here: 72.4 us
  Pallas kernels  69.8 us (96%)
  between operations  1.29 us (2%)
  local copies, waits for them, and re-layouts  1.28 us (2%)
    pallas_call x1, Pallas kernels, on_device(): pl.pallas_call(functools.partial(kernel, tp, sections, tok), out_shape=(p...  69.8 us

profile of v5, /device:TPU:33, one launch (start us, length us, event | category | flops | bytes accessed | tf_op | source)
XLA Modules:
  0.0 72.4 jit_solution(16268770552260349042)
XLA Ops:
  1.3 69.8 %shard_map.77 = (bf16[1,256,512]{2,1,0:T(8,128)(2,1)S(1)}, bf16[1,2,512]{2,1,0:T(2,128)(2,1)S(1)}) custom-call(bf16[1,256,512]{2,1,0:T(8,128)(2,1)} %x_hbm.1, bf16[1,512]{1,0:T(2,128)(2,1)} %gain_hbm.1, bf16[1,512,512]{2,1,0:T(8,128)(2,1)} %wv_hbm.1, bf16[1,512,512]{2,1,0:T(8,128)(2,1)} %wo_hbm.1, bf16[1,2,512]{2,1,0:T(2,128)(2,1)} %mom_hbm.1, ...), custom_call_target="tpu_custom_call" | custom-call | tf_op jit(solution)/shard_map/pallas_call | solution.py:289
  71.1 0.7 copy.10
  71.8 0.6 copy.11
